TPU v7x, 32 devices: a whole 2x2x4 slice. The times are simulated.
32 devices in a mesh: dp: 8 (over y, x, core), tensor: 4 (over z).
Axes of the slice: x: 2, y: 2, z: 4, core: 2. Of those that a mesh axis runs over, the one named last changes fastest.
Arguments:
- inputs: bfloat16 [2048, 2048], P(('dp', 'tensor')), parts along dimension 0, may hold values from -6 to 6
- grad_out: bfloat16 [2048, 2048], P(('dp', 'tensor')), parts along dimension 0, may hold values from -6 to 6
- gate_weight: bfloat16 [2048, 7168], P(None, 'tensor'), may hold values from -6 to 6
- up_weight: bfloat16 [2048, 7168], P(None, 'tensor'), may hold values from -6 to 6
- down_weight: bfloat16 [7168, 2048], P('tensor'), may hold values from -6 to 6
Outputs:
- grad_inputs: bfloat16 [2048, 2048], P(('dp', 'tensor')), parts along dimension 0
- grad_gate: bfloat16 [16384, 7168], P('dp', 'tensor'), parts along dimension 0
- grad_up: bfloat16 [16384, 7168], P('dp', 'tensor'), parts along dimension 0
- grad_down: bfloat16 [57344, 2048], P(('dp', 'tensor')), parts along dimension 0
There are 8 independent parts, one for each index of `dp`. A program takes and returns all parts, laid end to end along the dimension named above; an argument that names none is the same for every part. Nothing has to cross between parts.
All inputs are finite; a program needn't handle non-finite values.
Results may differ from a plain program's by a relative error of at most 0.0049.
Values may be sent and summed in bfloat16 or wider, within the bound.
A program may use at most 128 MiB of HBM per device.

v0:
```python
import jax
import jax.numpy as jnp
from jax import lax
from jax.sharding import PartitionSpec as P

D = 2048
FF = 7168


def contract_last(left, right):
    return lax.dot_general(
        left, right, (((1,), (1,)), ((), ())), preferred_element_type=jnp.float32
    )


def contract_first(left, right):
    return lax.dot_general(
        left, right, (((0,), (0,)), ((), ())), preferred_element_type=jnp.float32
    )


def on_device(inputs, grad_out, gate_weight, up_weight, down_weight):
    tokens_all = lax.all_gather(inputs, "tensor", axis=0, tiled=True)
    grads_all = lax.all_gather(grad_out, "tensor", axis=0, tiled=True)
    inv_width = D ** (-0.5)
    inv_rows = tokens_all.shape[0] ** (-0.5)
    inv_hidden = (2 * FF) ** (-0.5)
    gate = jnp.dot(tokens_all, gate_weight, preferred_element_type=jnp.float32) * inv_width
    up = jnp.dot(tokens_all, up_weight, preferred_element_type=jnp.float32) * inv_width
    sig = jax.nn.sigmoid(gate)
    act = gate * sig
    hidden = (act * up).astype(jnp.bfloat16)
    d_hidden = contract_last(grads_all, down_weight) * inv_width
    grad_down = (contract_first(hidden, grads_all) * inv_rows).astype(jnp.bfloat16)
    d_gate = (d_hidden * up * sig * (1.0 + gate * (1.0 - sig))).astype(jnp.bfloat16)
    d_up = (d_hidden * act).astype(jnp.bfloat16)
    grad_gate = (contract_first(tokens_all, d_gate) * inv_rows).astype(jnp.bfloat16)
    grad_up = (contract_first(tokens_all, d_up) * inv_rows).astype(jnp.bfloat16)
    summed = lax.psum_scatter(
        contract_last(d_gate, gate_weight) * inv_hidden
        + contract_last(d_up, up_weight) * inv_hidden,
        "tensor",
        scatter_dimension=0,
        tiled=True,
    )
    grad_inputs = summed.astype(jnp.bfloat16)
    return (grad_inputs, grad_gate, grad_up, grad_down)


def solution(mesh):
    placed = (
        P(("dp", "tensor"), None),
        P(("dp", "tensor"), None),
        P(None, "tensor"),
        P(None, "tensor"),
        P("tensor", None),
    )
    return jax.shard_map(
        on_device,
        mesh=mesh,
        in_specs=placed,
        out_specs=(
            P(("dp", "tensor"), None),
            P("dp", "tensor"),
            P("dp", "tensor"),
            P(("dp", "tensor"), None),
        ),
        check_vma=False,
    )
```

profile of v0, /device:TPU:0, one launch (start us, length us, event | category | flops | bytes accessed | tf_op | source)
XLA Modules:
  0.0 139.9 jit_solution(8619819542554499196)
XLA Ops:
  7.2 0.0 all-gather.5.cloned.1.call-start
  7.2 0.7 all-gather.5.cloned.1.call-update
  7.9 0.0 all-gather.3.cloned.1.call-start
  7.9 0.7 all-gather.3.cloned.1.call-update
  8.6 0.0 reduce-scatter.2.cloned.1.call-start
  8.7 31.5 %all-gather.5.cloned.1.call-done = bf16[256,2048]{1,0:T(8,128)(2,1)} async-done(((bf16[64,2048]{1,0:T(8,128)(2,1)}), bf16[256,2048]{1,0:T(8,128)(2,1)}) %all-gather.5.cloned.1.call-update) | async-done | bytes 1048592 | tf_op jit(solution)/shard_map/all_gather | solution.py:23
  40.2 0.0 copy-start
  40.2 6.8 %convolution_multiply_fusion = f32[256,1792]{1,0:T(8,128)} fusion(bf16[256,2048]{1,0:T(8,128)(2,1)} %all-gather.5.cloned.1.call-done, bf16[2048,1792]{1,0:T(8,128)(2,1)} %param.7), kind=kOutput, calls=%fused_computation.5 | convolution fusion | flops 1879506944 | bytes 10223616 | tf_op jit(solution)/shard_map/dot_general | solution.py:28
  47.0 0.0 copy-done
  47.0 6.6 %convolution_multiply_fusion.1 = f32[256,1792]{1,0:T(8,128)} fusion(bf16[256,2048]{1,0:T(8,128)(2,1)S(1)} %copy-done, bf16[2048,1792]{1,0:T(8,128)(2,1)} %param.8), kind=kOutput, calls=%fused_computation.6 | convolution fusion | flops 1879506944 | bytes 10223616 | tf_op jit(solution)/shard_map/dot_general | solution.py:29
  53.6 15.6 %all-gather.3.cloned.1.call-done = bf16[256,2048]{1,0:T(8,128)(2,1)} async-done(((bf16[64,2048]{1,0:T(8,128)(2,1)}), bf16[256,2048]{1,0:T(8,128)(2,1)}) %all-gather.3.cloned.1.call-update) | async-done | bytes 1048592 | tf_op jit(solution)/shard_map/all_gather | solution.py:24
  69.3 7.1 %multiply_convert_fusion.4 = (bf16[256,1792]{1,0:T(8,128)(2,1)S(1)}, bf16[256,1792]{1,0:T(8,128)(2,1)S(1)}) fusion(f32[256,1792]{1,0:T(8,128)} %convolution_multiply_fusion, f32[256,1792]{1,0:T(8,128)} %convolution_multiply_fusion.1, bf16[256,2048]{1,0:T(8,128)(2,1)} %all-gather.3.cloned.1.call-done, bf16[1792,2048]{1,0:T(8,128)(2,1)} %param.9), kind=kOutput, calls=%fused_computation.11 | convolution fusion | flops 1885470720 | bytes 13893632 | tf_op jit(solution)/shard_map/dot_general | solution.py:11
  76.3 5.2 %fusion.6 = f32[256,2048]{1,0:T(8,128)S(1)} fusion(bf16[256,1792]{1,0:T(8,128)(2,1)S(1)} %get-tuple-element.9, bf16[2048,1792]{1,0:T(8,128)(2,1)} %param.7), kind=kOutput, calls=%fused_computation.16 | convolution fusion | flops 1879048192 | bytes 10354688 | tf_op jit(solution)/shard_map/dot_general | solution.py:11
  81.5 6.6 %fusion.2 = f32[256,2048]{1,0:T(8,128)} fusion(f32[256,2048]{1,0:T(8,128)S(1)} %fusion.6, bf16[256,1792]{1,0:T(8,128)(2,1)S(1)} %get-tuple-element.8, bf16[2048,1792]{1,0:T(8,128)(2,1)} %param.8), kind=kOutput, calls=%fused_computation.9 | convolution fusion | flops 1880096768 | bytes 12451840 | tf_op jit(solution)/shard_map/dot_general | solution.py:11
  88.1 0.0 reduce-scatter.2.cloned.1.call-update
  88.1 5.2 %fusion.1 = bf16[2048,1792]{0,1:T(8,128)(2,1)} fusion(bf16[256,1792]{1,0:T(8,128)(2,1)S(1)} %get-tuple-element.8, bf16[256,2048]{1,0:T(8,128)(2,1)S(1)} %copy-done), kind=kOutput, calls=%fused_computation.4 | convolution fusion | flops 1886388224 | bytes 9306112 | tf_op jit(solution)/shard_map/dot_general | solution.py:17
  93.2 10.1 %copy.10 = bf16[2048,1792]{1,0:T(8,128)(2,1)} copy(bf16[2048,1792]{0,1:T(8,128)(2,1)} %fusion.1) | data formatting | bytes 14680064
  103.3 5.1 %fusion = bf16[2048,1792]{0,1:T(8,128)(2,1)} fusion(bf16[256,1792]{1,0:T(8,128)(2,1)S(1)} %get-tuple-element.9, bf16[256,2048]{1,0:T(8,128)(2,1)S(1)} %copy-done), kind=kOutput, calls=%fused_computation.3 | convolution fusion | flops 1886388224 | bytes 9306112 | tf_op jit(solution)/shard_map/dot_general | solution.py:17
  108.5 0.0 copy-start.1
  108.5 0.0 copy-start.2
  108.5 10.1 %copy.9 = bf16[2048,1792]{1,0:T(8,128)(2,1)} copy(bf16[2048,1792]{0,1:T(8,128)(2,1)} %fusion) | data formatting | bytes 14680064
  118.6 0.0 copy-done.1
  118.6 0.0 copy-done.2
  118.6 6.8 %multiply_convert_fusion = bf16[1792,2048]{1,0:T(8,128)(2,1)} fusion(bf16[256,2048]{1,0:T(8,128)(2,1)S(1)} %copy-done.1, f32[256,1792]{1,0:T(8,128)} %convolution_multiply_fusion.1, f32[256,1792]{1,0:T(8,128)S(1)} %copy-done.2), kind=kOutput, calls=%fused_computation | convolution fusion | flops 1889140736 | bytes 12058624 | tf_op jit(solution)/shard_map/dot_general | solution.py:17
  125.4 6.2 %reduce-scatter.2.cloned.1.call-done = f32[64,2048]{1,0:T(8,128)} async-done(((f32[256,2048]{1,0:T(8,128)}), f32[64,2048]{1,0:T(8,128)}) %reduce-scatter.2.cloned.1.call-update) | async-done | bytes 524304 | tf_op jit(solution)/shard_map/reduce_scatter | solution.py:39
  131.6 1.8 %convert_element_type.29 = bf16[64,2048]{1,0:T(8,128)(2,1)} convert(f32[64,2048]{1,0:T(8,128)} %reduce-scatter.2.cloned.1.call-done) | non-fusion elementwise | flops 131072 | bytes 786432 | tf_op jit(solution)/shard_map/convert_element_type | solution.py:46
Async XLA Ops:
  7.2 33.1 %all-gather.5.cloned.1.call-start = ((), (), s32[]{:S(2)}) async-start(), calls=%async_computation.2 | async-start | bytes 1310720 | tf_op jit(solution)/shard_map/all_gather | solution.py:23
  7.9 61.4 %all-gather.3.cloned.1.call-start = ((), (), s32[]{:S(2)}) async-start(), calls=%async_computation.1 | async-start | bytes 1310720 | tf_op jit(solution)/shard_map/all_gather | solution.py:24
  8.6 122.9 %reduce-scatter.2.cloned.1.call-start = ((), (), s32[]{:S(2)}) async-start(), calls=%async_computation.3 | async-start | bytes 2621440 | tf_op jit(solution)/shard_map/reduce_scatter | solution.py:39
  40.2 6.8 %copy-start = (bf16[256,2048]{1,0:T(8,128)(2,1)S(1)}, bf16[256,2048]{1,0:T(8,128)(2,1)}, u32[]{:S(2)}) copy-start(bf16[256,2048]{1,0:T(8,128)(2,1)} %all-gather.5.cloned.1.call-done) | copy-start | bytes 3145732
  108.5 10.1 %copy-start.1 = (bf16[256,2048]{1,0:T(8,128)(2,1)S(1)}, bf16[256,2048]{1,0:T(8,128)(2,1)}, u32[]{:S(2)}) copy-start(bf16[256,2048]{1,0:T(8,128)(2,1)} %all-gather.3.cloned.1.call-done) | copy-start | bytes 3145732
  108.5 10.1 %copy-start.2 = (f32[256,1792]{1,0:T(8,128)S(1)}, f32[256,1792]{1,0:T(8,128)}, u32[]{:S(2)}) copy-start(f32[256,1792]{1,0:T(8,128)} %convolution_multiply_fusion) | copy-start | bytes 5505028
Sparse Core Ops, SparseCore 0:
  9.6 30.6 all-gather.4
  41.8 27.4 all-gather.2
  88.2 43.3 reduce-scatter.1
where the time goes:
time: 141 us; the launch traced here: 140 us
  waiting for transfers between devices  54.7 us (39%)
  matrix products  49.3 us (35%)
  local copies, waits for them, and re-layouts  20.2 us (14%)
  between operations  13.8 us (10%)
  other arithmetic  1.77 us (1%)
    all_gather x1, waiting for transfers between devices, on_device(): tokens_all = lax.all_gather(inputs, 'tensor', axis=0, tiled=True)  31.5 us
    unnamed x8, local copies, waits for them, and re-layouts  20.2 us
    dot_general x3, matrix products, contract_last(): lax.dot_general(left, right, (((1,), (1,)), ((), ())), preferred_element_...  18.8 us
    dot_general x3, matrix products, contract_first(): lax.dot_general(left, right, (((0,), (0,)), ((), ())), preferred_element_...  17.1 us
    all_gather x1, waiting for transfers between devices, on_device(): grads_all = lax.all_gather(grad_out, 'tensor', axis=0, tiled=True)  15.6 us
    dot_general x1, matrix products, on_device(): jnp.dot(tokens_all, gate_weight, preferred_element_type=jnp.float32)  6.77 us
    dot_general x1, matrix products, on_device(): jnp.dot(tokens_all, up_weight, preferred_element_type=jnp.float32)  6.64 us
    reduce_scatter x1, waiting for transfers between devices, on_device(): lax.psum_scatter(contract_last(d_gate, gate_weight) * inv_hidden + contra...  6.19 us
  transfers between devices with their start and end apart: 3, of which 3 were waited for; matrix products, arithmetic and copies ran while one was open for 36% of the time, Pallas kernels for 0%

commit v1 on v0

--- a/solution.py
+++ b/solution.py
@@ -20,7 +20,13 @@
 
 
 def on_device(inputs, grad_out, gate_weight, up_weight, down_weight):
-    tokens_all = lax.all_gather(inputs, "tensor", axis=0, tiled=True)
+    devices = lax.axis_size("tensor")
+    current, blocks = (inputs, [inputs])
+    for _ in range(devices - 1):
+        current = lax.ppermute(current, "tensor", [(i, (i + 1) % devices) for i in range(devices)])
+        blocks.insert(0, current)
+    line = jnp.concatenate(blocks, axis=0)
+    tokens_all = jnp.roll(line, (lax.axis_index("tensor") + 1) * inputs.shape[0], axis=0)
     grads_all = lax.all_gather(grad_out, "tensor", axis=0, tiled=True)
     inv_width = D ** (-0.5)
     inv_rows = tokens_all.shape[0] ** (-0.5)

time: 141 us -> 129 us (0.915)
  local copies, waits for them, and re-layouts: 20.2 us -> 1.16 us
  waiting for transfers between devices: 54.7 us -> 62.3 us
  starting transfers between devices: 0.11 us -> 3.16 us
  matrix products: 49.3 us -> 46.5 us
    all_gather x1 -> x0, waiting for transfers between devices: 31.5 us -> none  [on_device(): tokens_all = lax.all_gather(inputs, 'tensor', axis=0, tiled=True)]
    ppermute x0 -> x3, waiting for transfers between devices: none -> 26.1 us  [on_device(): lax.ppermute(current, 'tensor', [(i, (i + 1) % devices) for i in range(de...]
    reduce_scatter x1, waiting for transfers between devices: 6.19 us -> 26.3 us  [on_device(): lax.psum_scatter(contract_last(d_gate, gate_weight) * inv_hidden + contra...]
    unnamed x8 -> x25, local copies, waits for them, and re-layouts: 20.2 us -> 1.14 us
    all_gather x1, waiting for transfers between devices: 15.6 us -> 9.89 us  [on_device(): grads_all = lax.all_gather(grad_out, 'tensor', axis=0, tiled=True)]
    dot_general x1, matrix products: 6.64 us -> 3.34 us  [on_device(): jnp.dot(tokens_all, up_weight, preferred_element_type=jnp.float32)]
    ppermute x0 -> x3, starting transfers between devices: none -> 3.08 us  [on_device(): lax.ppermute(current, 'tensor', [(i, (i + 1) % devices) for i in range(de...]
  transfers between devices with their start and end apart: 3 -> 5, of which waited for: 3 -> 5; matrix products, arithmetic and copies ran while one was open for 36% -> 22% of each run, Pallas kernels for 0% -> 0%
where the time goes in v1:
time: 129 us
  waiting for transfers between devices  62.3 us (48%)
  matrix products  46.5 us (36%)
  between operations  14.2 us (11%)
  starting transfers between devices  3.16 us (2%)
  other arithmetic  1.77 us (1%)
    reduce_scatter x1, waiting for transfers between devices, on_device(): lax.psum_scatter(contract_last(d_gate, gate_weight) * inv_hidden + contra...  26.3 us
    ppermute x3, waiting for transfers between devices, on_device(): lax.ppermute(current, 'tensor', [(i, (i + 1) % devices) for i in range(de...  26.1 us
    dot_general x3, matrix products, contract_last(): lax.dot_general(left, right, (((1,), (1,)), ((), ())), preferred_element_...  19.4 us
    dot_general x3, matrix products, contract_first(): lax.dot_general(left, right, (((0,), (0,)), ((), ())), preferred_element_...  17.2 us
    all_gather x1, waiting for transfers between devices, on_device(): grads_all = lax.all_gather(grad_out, 'tensor', axis=0, tiled=True)  9.89 us
    dot_general x1, matrix products, on_device(): jnp.dot(tokens_all, gate_weight, preferred_element_type=jnp.float32)  6.54 us
    dot_general x1, matrix products, on_device(): jnp.dot(tokens_all, up_weight, preferred_element_type=jnp.float32)  3.34 us
    ppermute x3, starting transfers between devices, on_device(): lax.ppermute(current, 'tensor', [(i, (i + 1) % devices) for i in range(de...  3.08 us
  transfers between devices with their start and end apart: 5, of which 5 were waited for; matrix products, arithmetic and copies ran while one was open for 22% of the time, Pallas kernels for 0%

profile of v1, /device:TPU:0, one launch (start us, length us, event | category | flops | bytes accessed | tf_op | source)
XLA Modules:
  0.0 129.1 jit_solution(11981346091494282228)
XLA Ops:
  7.2 0.0 copy-start
  7.2 0.0 all-gather.2.cloned.1.call-start
  7.2 3.1 %collective-permute-start = (bf16[64,2048]{1,0:T(8,128)(2,1)}, bf16[64,2048]{1,0:T(8,128)(2,1)S(1)}, u32[]{:S(2)}, u32[]{:S(2)}) collective-permute-start(bf16[64,2048]{1,0:T(8,128)(2,1)} %param.5), channel_id=1, source_target_pairs={{0,1},{1,2},{2,3},{3,0},{4,5},{5,6},{6,7},{7,4},{8,9},{9,10},{10,1... | collective-permute-start | bytes 786440 | tf_op jit(solution)/shard_map/ppermute | solution.py:26
  10.3 8.5 %collective-permute-done = bf16[64,2048]{1,0:T(8,128)(2,1)S(1)} collective-permute-done((bf16[64,2048]{1,0:T(8,128)(2,1)}, bf16[64,2048]{1,0:T(8,128)(2,1)S(1)}, u32[]{:S(2)}, u32[]{:S(2)}) %collective-permute-start) | collective-permute-done | bytes 262176 | tf_op jit(solution)/shard_map/ppermute | solution.py:26
  18.8 0.0 collective-permute-start.1
  18.8 9.3 %collective-permute-done.1 = bf16[64,2048]{1,0:T(8,128)(2,1)S(1)} collective-permute-done((bf16[64,2048]{1,0:T(8,128)(2,1)S(1)}, bf16[64,2048]{1,0:T(8,128)(2,1)S(1)}, u32[]{:S(2)}, u32[]{:S(2)}) %collective-permute-start.1) | collective-permute-done | bytes 262176 | tf_op jit(solution)/shard_map/ppermute | solution.py:26
  28.1 0.0 collective-permute-start.2
  28.1 0.0 all-gather.2.cloned.1.call-update
  28.2 0.0 reduce-scatter.2.cloned.1.call-start
  28.2 8.3 %collective-permute-done.2 = bf16[64,2048]{1,0:T(8,128)(2,1)S(1)} collective-permute-done((bf16[64,2048]{1,0:T(8,128)(2,1)S(1)}, bf16[64,2048]{1,0:T(8,128)(2,1)S(1)}, u32[]{:S(2)}, u32[]{:S(2)}) %collective-permute-start.2) | collective-permute-done | bytes 262176 | tf_op jit(solution)/shard_map/ppermute | solution.py:26
  36.6 1.0 constant_dynamic-update-slice_fusion.4
  37.6 0.0 copy-done
  37.6 0.0 slice-start
  37.7 0.0 slice-start.1
  37.7 6.5 %convolution_multiply_fusion = f32[256,1792]{1,0:T(8,128)} fusion(bf16[2048,1792]{1,0:T(8,128)(2,1)} %param.7, bf16[512,2048]{1,0:T(8,128)(2,1)S(1)} %constant_dynamic-update-slice_fusion, s32[]{:T(128)S(6)} %select_n.14), kind=kOutput, calls=%fused_computation.3 | convolution fusion | flops 1879506944 | bytes 10223620 | tf_op jit(solution)/shard_map/dot_general | solution.py:34
  44.2 0.0 slice-done
  44.2 0.0 slice-done.1
  44.2 3.3 %convolution_multiply_fusion.1 = f32[256,1792]{1,0:T(8,128)} fusion(bf16[2048,1792]{1,0:T(8,128)(2,1)S(1)} %bitcast.12, bf16[512,2048]{1,0:T(8,128)(2,1)S(1)} %constant_dynamic-update-slice_fusion, s32[]{:T(128)S(6)} %select_n.14), kind=kOutput, calls=%fused_computation.4 | convolution fusion | flops 1879506944 | bytes 10223620 | tf_op jit(solution)/shard_map/dot_general | solution.py:35
  47.6 9.9 %all-gather.2.cloned.1.call-done = bf16[256,2048]{1,0:T(8,128)(2,1)} async-done(((bf16[64,2048]{1,0:T(8,128)(2,1)}), bf16[256,2048]{1,0:T(8,128)(2,1)}) %all-gather.2.cloned.1.call-update) | async-done | bytes 1048592 | tf_op jit(solution)/shard_map/all_gather | solution.py:30
  57.5 7.0 %multiply_convert_fusion.4 = (bf16[256,1792]{1,0:T(8,128)(2,1)S(1)}, bf16[256,1792]{1,0:T(8,128)(2,1)S(1)}) fusion(f32[256,1792]{1,0:T(8,128)} %convolution_multiply_fusion, f32[256,1792]{1,0:T(8,128)} %convolution_multiply_fusion.1, bf16[256,2048]{1,0:T(8,128)(2,1)} %all-gather.2.cloned.1.call-done, bf16[1792,2048]{1,0:T(8,128)(2,1)} %param.9), kind=kOutput, calls=%fused_computation.9 | convolution fusion | flops 1885470720 | bytes 13893632 | tf_op jit(solution)/shard_map/dot_general | solution.py:11
  64.5 0.0 copy-start.3
  64.5 0.0 copy-start.2
  64.6 5.8 %fusion.12 = f32[256,2048]{1,0:T(8,128)S(1)} fusion(bf16[256,1792]{1,0:T(8,128)(2,1)S(1)} %get-tuple-element.5, bf16[2048,1792]{1,0:T(8,128)(2,1)} %param.7), kind=kOutput, calls=%fused_computation.30 | convolution fusion | flops 1879048192 | bytes 10354688 | tf_op jit(solution)/shard_map/dot_general | solution.py:11
  70.4 0.0 copy-done.3
  70.4 0.0 copy-done.2
  70.4 6.6 %fusion = f32[256,2048]{1,0:T(8,128)} fusion(f32[256,2048]{1,0:T(8,128)S(1)} %fusion.12, bf16[256,1792]{1,0:T(8,128)(2,1)S(1)} %get-tuple-element.4, bf16[2048,1792]{1,0:T(8,128)(2,1)} %param.8), kind=kOutput, calls=%fused_computation.7 | convolution fusion | flops 1880096768 | bytes 12451840 | tf_op jit(solution)/shard_map/dot_general | solution.py:11
  77.0 0.0 reduce-scatter.2.cloned.1.call-update
  77.0 0.0 copy-start.4
  77.0 6.4 %multiply_convert_fusion.1 = bf16[2048,1792]{1,0:T(8,128)(2,1)} fusion(bf16[256,1792]{1,0:T(8,128)(2,1)} %copy-done.2, bf16[512,2048]{1,0:T(8,128)(2,1)S(1)} %constant_dynamic-update-slice_fusion, s32[]{:T(128)S(6)} %select_n.14), kind=kOutput, calls=%fused_computation.1 | convolution fusion | flops 1886388224 | bytes 9306116 | tf_op jit(solution)/shard_map/dot_general | solution.py:17
  83.5 0.0 copy-done.4
  83.5 0.0 copy-start.1
  83.5 0.0 copy-start.5
  83.5 0.0 copy-start.6
  83.5 5.4 %multiply_convert_fusion.2 = bf16[2048,1792]{1,0:T(8,128)(2,1)} fusion(bf16[256,1792]{1,0:T(8,128)(2,1)S(1)} %copy-done.4, bf16[512,2048]{1,0:T(8,128)(2,1)S(1)} %constant_dynamic-update-slice_fusion, s32[]{:T(128)S(6)} %select_n.14), kind=kOutput, calls=%fused_computation.2 | convolution fusion | flops 1886388224 | bytes 9306116 | tf_op jit(solution)/shard_map/dot_general | solution.py:17
  88.9 0.0 copy-done.1
  88.9 0.0 copy-done.5
  88.9 0.0 copy-done.6
  88.9 5.4 %multiply_convert_fusion = bf16[1792,2048]{1,0:T(8,128)(2,1)} fusion(bf16[256,2048]{1,0:T(8,128)(2,1)S(1)} %copy-done.1, f32[256,1792]{1,0:T(8,128)S(1)} %copy-done.6, f32[256,1792]{1,0:T(8,128)S(1)} %copy-done.5), kind=kOutput, calls=%fused_computation | convolution fusion | flops 1889140736 | bytes 12058624 | tf_op jit(solution)/shard_map/dot_general | solution.py:17
  94.2 26.3 %reduce-scatter.2.cloned.1.call-done = f32[64,2048]{1,0:T(8,128)} async-done(((f32[256,2048]{1,0:T(8,128)}), f32[64,2048]{1,0:T(8,128)}) %reduce-scatter.2.cloned.1.call-update) | async-done | bytes 524304 | tf_op jit(solution)/shard_map/reduce_scatter | solution.py:45
  120.5 1.8 %convert_element_type.23 = bf16[64,2048]{1,0:T(8,128)(2,1)} convert(f32[64,2048]{1,0:T(8,128)} %reduce-scatter.2.cloned.1.call-done) | non-fusion elementwise | flops 131072 | bytes 786432 | tf_op jit(solution)/shard_map/convert_element_type | solution.py:52
  (8 shorter events, 0.1 us)
Async XLA Ops:
  7.2 30.5 %copy-start = (bf16[64,2048]{1,0:T(8,128)(2,1)S(1)}, bf16[64,2048]{1,0:T(8,128)(2,1)}, u32[]{:S(2)}) copy-start(bf16[64,2048]{1,0:T(8,128)(2,1)} %param.5) | copy-start | bytes 786436
  7.2 50.3 %all-gather.2.cloned.1.call-start = ((), (), s32[]{:S(2)}) async-start(), calls=%async_computation.1 | async-start | bytes 1310720 | tf_op jit(solution)/shard_map/all_gather | solution.py:30
  7.2 11.6 %collective-permute-start = (bf16[64,2048]{1,0:T(8,128)(2,1)}, bf16[64,2048]{1,0:T(8,128)(2,1)S(1)}, u32[]{:S(2)}, u32[]{:S(2)}) collective-permute-start(bf16[64,2048]{1,0:T(8,128)(2,1)} %param.5), channel_id=1, source_target_pairs={{0,1},{1,2},{2,3},{3,0},{4,5},{5,6},{6,7},{7,4},{8,9},{9,10},{10,1... | collective-permute-start | bytes 786440 | tf_op jit(solution)/shard_map/ppermute | solution.py:26
  18.8 9.3 %collective-permute-start.1 = (bf16[64,2048]{1,0:T(8,128)(2,1)S(1)}, bf16[64,2048]{1,0:T(8,128)(2,1)S(1)}, u32[]{:S(2)}, u32[]{:S(2)}) collective-permute-start(bf16[64,2048]{1,0:T(8,128)(2,1)S(1)} %collective-permute-done), channel_id=1, source_target_pairs={{0,1},{1,2},{2,3},{3,0},{4,5},{5,6},{6,7},{7,4},{8,9},{9,10},{10,1... | collective-permute-start | bytes 786440 | tf_op jit(solution)/shard_map/ppermute | solution.py:26
  28.1 8.4 %collective-permute-start.2 = (bf16[64,2048]{1,0:T(8,128)(2,1)S(1)}, bf16[64,2048]{1,0:T(8,128)(2,1)S(1)}, u32[]{:S(2)}, u32[]{:S(2)}) collective-permute-start(bf16[64,2048]{1,0:T(8,128)(2,1)S(1)} %collective-permute-done.1), channel_id=1, source_target_pairs={{0,1},{1,2},{2,3},{3,0},{4,5},{5,6},{6,7},{7,4},{8,9},{9,10},{10,1... | collective-permute-start | bytes 786440 | tf_op jit(solution)/shard_map/ppermute | solution.py:26
  28.2 92.4 %reduce-scatter.2.cloned.1.call-start = ((), (), s32[]{:S(2)}) async-start(), calls=%async_computation.2 | async-start | bytes 2621440 | tf_op jit(solution)/shard_map/reduce_scatter | solution.py:45
  37.6 6.6 %slice-start = ((s8[7340032]{0:T(1024)(128)(4,1)}), s8[4194304]{0:T(1024)(128)(4,1)S(1)}, s32[]{:S(2)}) async-start(s8[7340032]{0:T(1024)(128)(4,1)} %bitcast.11), calls=%async_computation.3 | async-start | bytes 8388608
  37.7 6.6 %slice-start.1 = ((s8[7340032]{0:T(1024)(128)(4,1)}), s8[3145728]{0:T(1024)(128)(4,1)S(1)}, s32[]{:S(2)}) async-start(s8[7340032]{0:T(1024)(128)(4,1)} %bitcast.11), calls=%async_computation.4 | async-start | bytes 6291456
  64.5 5.9 %copy-start.3 = (bf16[256,1792]{1,0:T(8,128)(2,1)}, bf16[256,1792]{1,0:T(8,128)(2,1)S(1)}, u32[]{:S(2)}) copy-start(bf16[256,1792]{1,0:T(8,128)(2,1)S(1)} %get-tuple-element.5) | copy-start | bytes 2752516
  64.5 5.9 %copy-start.2 = (bf16[256,1792]{1,0:T(8,128)(2,1)}, bf16[256,1792]{1,0:T(8,128)(2,1)S(1)}, u32[]{:S(2)}) copy-start(bf16[256,1792]{1,0:T(8,128)(2,1)S(1)} %get-tuple-element.4) | copy-start | bytes 2752516
  77.0 6.5 %copy-start.4 = (bf16[256,1792]{1,0:T(8,128)(2,1)S(1)}, bf16[256,1792]{1,0:T(8,128)(2,1)}, u32[]{:S(2)}) copy-start(bf16[256,1792]{1,0:T(8,128)(2,1)} %copy-done.3) | copy-start | bytes 2752516
  83.5 5.4 %copy-start.1 = (bf16[256,2048]{1,0:T(8,128)(2,1)S(1)}, bf16[256,2048]{1,0:T(8,128)(2,1)}, u32[]{:S(2)}) copy-start(bf16[256,2048]{1,0:T(8,128)(2,1)} %all-gather.2.cloned.1.call-done) | copy-start | bytes 3145732
  83.5 5.4 %copy-start.5 = (f32[256,1792]{1,0:T(8,128)S(1)}, f32[256,1792]{1,0:T(8,128)}, u32[]{:S(2)}) copy-start(f32[256,1792]{1,0:T(8,128)} %convolution_multiply_fusion) | copy-start | bytes 5505028
  83.5 5.4 %copy-start.6 = (f32[256,1792]{1,0:T(8,128)S(1)}, f32[256,1792]{1,0:T(8,128)}, u32[]{:S(2)}) copy-start(f32[256,1792]{1,0:T(8,128)} %convolution_multiply_fusion.1) | copy-start | bytes 5505028
Sparse Core Ops, SparseCore 0:
  28.3 29.1 all-gather.1
  77.1 43.3 reduce-scatter.1
